TPU v7x, 256 devices: a whole 4x4x8 slice. The times are simulated.
256 devices in a mesh: bead: 32 (over y, z), space: 8 (over x, core).
Axes of the slice: x: 4, y: 4, z: 8, core: 2. Of those that a mesh axis runs over, the one named last changes fastest.
Arguments:
- positions: float32 [32, 3, 131072], P('bead', None, 'space'), may hold values from -5.5 to 5.5
- charges: float32 [131072], P('space'), may hold values from -1 to 1
- polarizability: float32 [131072], P('space'), may hold values from 0.03 to 0.12
- masses: float32 [131072], P('space'), may hold values from 1 to 16
- neighbors: int32 [1024, 8], P('space'), may hold values from 0 to 135, as said below
Outputs:
- forces: float32 [32, 3, 131072], P('bead', None, 'space')
- dipoles: float32 [3, 131072], P(None, ('space', 'bead'))
Inputs may be any that keep to these rules, and one draw needn't show every extreme that they name: `neighbors`: row t lists 8 different tiles by their index in its domain's extended numbering: the last 4 tiles of the previous domain, the domain's own 128 tiles, the first 4 tiles of the next domain (domains form a cycle). Every listed tile lies within 4 tiles of tile t, and the two tiles at distance exactly 4 on either side are always listed.
All inputs are finite; a program needn't handle non-finite values.
Results may differ from a plain program's by a relative error of at most 0.0001.
Values sent between devices are 32-bit elements; how exact they have to be, the bound alone decides.
No kernel may reach another device: no remote copies, remote signals or barrier semaphores. Data moves between devices by JAX's collectives and lax.ppermute only.
A program may use at most 64 MiB of HBM per device.

v0:
```python
import math
import jax
import jax.numpy as jnp
from jax import lax
from jax.sharding import PartitionSpec as P

TILE = 128
HALO_T = 4
ITERS = 3
REPULSION = 0.2
SPRING = 0.1


def extended_2(value, sides, width):
    for axis, dim in sides:
        size, length = (lax.axis_size(axis), value.shape[dim])
        up = [(i, (i + 1) % size) for i in range(size)]
        down = [(j, i) for i, j in up]
        last = lax.slice_in_dim(value, length - width, length, axis=dim)
        first = lax.slice_in_dim(value, 0, width, axis=dim)
        before = lax.ppermute(last, axis, up)
        after = lax.ppermute(first, axis, down)
        value = jnp.concatenate([before, value, after], axis=dim)
    return value


def repulsion_kernel(targets, sources):
    displace = targets[:, :, :, None] - sources[:, :, None, :]
    weight = jnp.exp(-0.5 * jnp.sum(displace * displace, axis=0))
    return REPULSION * jnp.sum(weight[None] * displace, axis=3)


def charge_kernel(targets, sources, charge):
    displace = targets[:, :, :, None] - sources[:, :, None, :]
    weight = jnp.exp(-0.25 * jnp.sum(displace * displace, axis=0)) * charge[0][:, None, :]
    return jnp.sum(weight[None] * displace, axis=3)


def dipole_kernel(targets, sources, dipole):
    displace = targets[:, :, :, None] - sources[:, :, None, :]
    weight = jnp.exp(-0.25 * jnp.sum(displace * displace, axis=0))
    spread_dip = dipole[:, :, None, :]
    projected = jnp.sum(displace * spread_dip, axis=0)
    return jnp.sum(weight[None] * (0.25 * displace * projected[None] - 0.5 * spread_dip), axis=3)


def grouped(kernel, targets, sources):
    tile_count = targets.shape[1]
    group_size = math.gcd(tile_count, 4)

    def split_tiles(tensor):
        return jnp.moveaxis(
            tensor.reshape(tensor.shape[0], tile_count // group_size, group_size, tensor.shape[2]),
            1,
            0,
        )

    pieces = tuple((split_tiles(tensor) for tensor in (targets,) + tuple(sources)))
    result = lax.map(lambda member: kernel(*member), pieces)
    return jnp.moveaxis(result, 0, 1).reshape(3, tile_count, targets.shape[2])


def gather_local(extended, tile_rows):
    channels = extended.shape[0]
    tiles = extended.reshape(channels, extended.shape[1] // TILE, TILE)
    picked = jnp.take(tiles, tile_rows, axis=1)
    return picked.reshape(channels, tile_rows.shape[0], tile_rows.shape[1] * TILE)


def per_device(positions, charges, polarizability, masses, neighbors):
    coords = positions[0]
    atom_dev = coords.shape[1]
    rim_width = HALO_T * TILE
    tiles_domain = atom_dev // TILE
    beads = lax.axis_size("bead")
    bead_index = lax.axis_index("bead")
    own_tiles = tiles_domain // beads
    own_start = bead_index * own_tiles
    cycle_rows = extended_2(positions, (("bead", 0),), 1)
    spring = SPRING * masses[None, :] * (cycle_rows[0] + cycle_rows[2] - 2.0 * coords)
    extended = extended_2(coords, (("space", 1),), rim_width)
    targets = coords.reshape(3, tiles_domain, TILE)
    short_range = grouped(repulsion_kernel, targets, (gather_local(extended, neighbors),)).reshape(
        3, atom_dev
    )
    centroid = lax.psum(coords, "bead") / beads
    with_charge = jnp.concatenate([centroid, charges[None]], axis=0)
    cent_ext = extended_2(with_charge, (("space", 1),), rim_width)
    cent_tiles = centroid.reshape(3, tiles_domain, TILE)
    cent_sources = gather_local(cent_ext[:3], neighbors)
    charge_sources = gather_local(cent_ext[3:], neighbors)
    permanent = grouped(charge_kernel, cent_tiles, (cent_sources, charge_sources)).reshape(
        3, atom_dev
    )

    def induced(dipole_all):
        wide_dip = extended_2(dipole_all, (("space", 1),), rim_width)
        field = grouped(
            dipole_kernel, cent_tiles, (cent_sources, gather_local(wide_dip, neighbors))
        )
        return field.reshape(3, atom_dev)

    domain_dip = polarizability[None] * permanent
    for sweep_index in range(ITERS):
        domain_dip = polarizability[None] * (permanent + induced(domain_dip))
    pulled = charges[None] * induced(domain_dip)
    dipoles = lax.dynamic_slice_in_dim(domain_dip, own_start * TILE, own_tiles * TILE, 1)
    forces = (short_range + spring + pulled)[None]
    return (forces, dipoles)


def solution(mesh):
    in_specs = (P("bead", None, "space"), P("space"), P("space"), P("space"), P("space", None))
    out_specs = (P("bead", None, "space"), P(None, ("space", "bead")))
    return jax.shard_map(
        per_device, mesh=mesh, in_specs=in_specs, out_specs=out_specs, check_vma=False
    )
```

profile of v0, /device:TPU:7, one launch (start us, length us, event | category | flops | bytes accessed | tf_op | source)
XLA Modules:
  0.0 1015.9 jit_solution(263732601985356042)
XLA Ops:
  8.3 2.5 collective-permute-start
  11.6 3.4 collective-permute-done.1
  15.9 145.2 %all-reduce.2.cloned.1.call-done = f32[3,16384]{1,0:T(4,128)} async-done(((f32[3,16384]{1,0:T(4,128)}), f32[3,16384]{1,0:T(4,128)}) %all-reduce.2.cloned.1.call-update) | async-done | bytes 196624 | tf_op jit(solution)/shard_map/psum | solution.py:86
  162.8 5.3 collective-permute-start.4
  169.2 3.6 gather_fusion.1
  173.3 2.8 gather_fusion
  177.1 8.0 gather_fusion.2
  185.1 3.6 fusion.29
  188.7 1.8 reshape_reshape.50
  192.1 87.0 %while.61 = (s32[]{:T(128)}, f32[32,3,4,128]{3,2,1,0:T(4,128)S(1)}, f32[32,3,4,128]{3,2,1,0:T(4,128)S(1)}, f32[32,3,4,1024]{3,2,1,0:T(4,128)}, f32[32,1,4,1024]{3,2,1,0:T(4,128)S(1)}, /*index=5*/s32[]{:T(128)}) while((s32[]{:T(128)}, f32[32,3,4,128]{3,2,1,0:T(4,128)S(1)}, f32[32,3,4,128]{3,2,1,0:T(4,128)S(1)}, f32[32,3,4,1024]{3,2,1,0:T(4,128)}, ...), condition=%wide.region_8.10_spmd, body=%wide.region_5.9_spmd.sunk | while | flops 9959938 | bytes 8677469 | solution.py:59
  279.3 3.0 collective-permute-start.6
  283.1 3.5 collective-permute-done.7
  286.7 3.6 gather_fusion.3
  291.6 1.8 reshape_reshape.52
  293.5 141.8 %while.62 = (s32[]{:T(128)}, f32[32,3,4,128]{3,2,1,0:T(4,128)S(1)}, f32[32,3,4,128]{3,2,1,0:T(4,128)S(1)}, f32[32,3,4,1024]{3,2,1,0:T(4,128)}, f32[32,3,4,1024]{3,2,0,1:T(4,128)S(1)}, /*index=5*/s32[]{:T(128)}) while((s32[]{:T(128)}, f32[32,3,4,128]{3,2,1,0:T(4,128)S(1)}, f32[32,3,4,128]{3,2,1,0:T(4,128)S(1)}, ...), condition=%wide.region_13.15_spmd, body=%wide.region_9.14_spmd.sunk | while | flops 15739394 | bytes 17262684 | solution.py:59
  340.6 1.6 fusion.51
  436.5 4.4 collective-permute-start.3
  441.0 3.6 gather_fusion.4
  446.0 1.8 reshape_reshape.54
  447.8 141.8 %while.63 = (s32[]{:T(128)}, f32[32,3,4,128]{3,2,1,0:T(4,128)S(1)}, f32[32,3,4,128]{3,2,1,0:T(4,128)S(1)}, f32[32,3,4,1024]{3,2,1,0:T(4,128)}, f32[32,3,4,1024]{3,2,0,1:T(4,128)S(1)}, /*index=5*/s32[]{:T(128)}) while((s32[]{:T(128)}, f32[32,3,4,128]{3,2,1,0:T(4,128)S(1)}, f32[32,3,4,128]{3,2,1,0:T(4,128)S(1)}, ...), condition=%wide.region_18.20_spmd, body=%wide.region_14.19_spmd.sunk | while | flops 15739394 | bytes 17262684 | solution.py:59
  590.0 3.1 collective-permute-start.10
  593.0 1.7 reshape_reshape.47
  594.7 2.6 collective-permute-done.11
  597.4 3.6 gather_fusion.5
  602.3 1.8 reshape_reshape.56
  604.1 141.8 %while.64 = (s32[]{:T(128)}, f32[32,3,4,128]{3,2,1,0:T(4,128)S(1)}, f32[32,3,4,128]{3,2,1,0:T(4,128)S(1)}, f32[32,3,4,1024]{3,2,1,0:T(4,128)}, f32[32,3,4,1024]{3,2,0,1:T(4,128)S(1)}, /*index=5*/s32[]{:T(128)}) while((s32[]{:T(128)}, f32[32,3,4,128]{3,2,1,0:T(4,128)S(1)}, f32[32,3,4,128]{3,2,1,0:T(4,128)S(1)}, ...), condition=%wide.region_23.25_spmd, body=%wide.region_19.24_spmd.sunk | while | flops 15739394 | bytes 17262684 | solution.py:59
  746.9 3.0 collective-permute-start.12
  749.9 107.9 %while.60 = (s32[]{:T(128)}, f32[32,3,4,128]{3,2,1,0:T(4,128)S(1)}, f32[32,3,4,128]{3,2,0,1:T(4,128)}, f32[32,3,4,1024]{3,2,0,1:T(4,128)}, s32[]{:T(128)}) while((s32[]{:T(128)}, f32[32,3,4,128]{3,2,1,0:T(4,128)S(1)}, f32[32,3,4,128]{3,2,0,1:T(4,128)}, f32[32,3,4,1024]{3,2,0,1:T(4,128)}, s32[]{:T(128)}) %tuple.164), condition=%wide.region_3.5_spmd, body=%wide.region_0.4_spmd.sunk | while | flops 9437186 | bytes 8628305 | solution.py:59
  857.9 3.6 gather_fusion.6
  862.9 1.8 reshape_reshape.58
  864.7 142.0 %while.65 = (s32[]{:T(128)}, f32[32,3,4,128]{3,2,1,0:T(4,128)S(1)}, f32[32,3,4,128]{3,2,1,0:T(4,128)S(1)}, f32[32,3,4,1024]{3,2,1,0:T(4,128)}, f32[32,3,4,1024]{3,2,0,1:T(4,128)S(1)}, /*index=5*/s32[]{:T(128)}) while((s32[]{:T(128)}, f32[32,3,4,128]{3,2,1,0:T(4,128)S(1)}, f32[32,3,4,128]{3,2,1,0:T(4,128)S(1)}, ...), condition=%wide.region_28.30_spmd, body=%wide.region_24.29_spmd.sunk | while | flops 15739394 | bytes 17262684 | solution.py:59
  1006.8 2.2 multiply_add_fusion
  (1402 shorter events, 769.6 us)
Async XLA Ops:
  7.2 160.9 %copy-start.7 = (s32[128,8]{0,1:T(8,128)S(1)}, s32[128,8]{0,1:T(8,128)}, u32[]{:S(2)}) copy-start(s32[128,8]{0,1:T(8,128)} %param.23) | copy-start | bytes 12292
  8.2 6.9 copy-start.1
  8.3 3.4 collective-permute-start
  10.7 4.3 collective-permute-start.1
  15.1 146.0 %all-reduce.2.cloned.1.call-start = ((), (), s32[]{:S(2)}) async-start(), calls=%async_computation | async-start | bytes 524288 | tf_op jit(solution)/shard_map/psum | solution.py:86
  162.8 10.2 collective-permute-start.4
  168.1 4.9 collective-permute-start.5
  169.2 3.8 copy-start.3
  190.5 1.3 copy-start.2
  190.5 1.3 copy-start.5
  192.1 87.2 %copy-start.4 = (f32[16384]{0:T(1024)S(1)}, f32[16384]{0:T(1024)}, u32[]{:S(2)}) copy-start(f32[16384]{0:T(1024)} %param.21) | copy-start | bytes 196612
  279.3 3.8 collective-permute-start.6
  282.3 4.3 collective-permute-start.7
  435.6 5.3 collective-permute-start.8
  435.7 5.3 collective-permute-start.9
  436.1 570.7 %collective-permute-start.2 = (f32[1,3,16384]{2,0,1:T(1,128)}, f32[1,3,16384]{2,0,1:T(1,128)S(1)}, u32[]{:S(2)}, u32[]{:S(2)}) collective-permute-start(f32[1,3,16384]{2,0,1:T(1,128)} %param.19), channel_id=1, source_target_pairs={{0,8},{8,16},{16,24},{24,32},{32,40},{40,48},{48,56},{56,64},{64,7... | collective-permute-start | bytes 589832 | tf_op jit(solution)/shard_map/ppermute | solution.py:21
  436.5 570.3 %collective-permute-start.3 = (f32[1,3,16384]{2,0,1:T(1,128)}, f32[1,3,16384]{2,0,1:T(1,128)}, u32[]{:S(2)}, u32[]{:S(2)}) collective-permute-start(f32[1,3,16384]{2,0,1:T(1,128)} %param.19), channel_id=1, source_target_pairs={{8,0},{16,8},{24,16},{32,24},{40,32},{48,40},{56,48},{64,56},{72,6... | collective-permute-start | bytes 589832 | tf_op jit(solution)/shard_map/ppermute | solution.py:22
  447.8 145.2 %copy-start.6 = (f32[16384]{0:T(1024)S(1)}, f32[16384]{0:T(1024)}, u32[]{:S(2)}) copy-start(f32[16384]{0:T(1024)} %param.22) | copy-start | bytes 196612
  589.6 3.4 copy-start
  590.0 4.7 collective-permute-start.10
  593.0 4.3 collective-permute-start.11
  746.9 111.0 %collective-permute-start.13 = (f32[3,512]{1,0:T(4,128)S(1)}, f32[3,512]{1,0:T(4,128)S(1)}, u32[]{:S(2)}, u32[]{:S(2)}) collective-permute-start(f32[3,512]{1,0:T(4,128)S(1)} %get-tuple-element.309), channel_id=1, source_target_pairs={{1,0},{2,1},{3,2},{4,3},{5,4},{6,5},{7,6},{0,7},{9,8},{10,9},{11,1... | collective-permute-start | bytes 18440 | tf_op jit(solution)/shard_map/ppermute | solution.py:22
  746.9 111.0 %collective-permute-start.12 = (f32[3,512]{1,0:T(4,128)S(1)}, f32[3,512]{1,0:T(4,128)S(1)}, u32[]{:S(2)}, u32[]{:S(2)}) collective-permute-start(f32[3,512]{1,0:T(4,128)S(1)} %get-tuple-element.310), channel_id=1, source_target_pairs={{0,1},{1,2},{2,3},{3,4},{4,5},{5,6},{6,7},{7,0},{8,9},{9,10},{10,1... | collective-permute-start | bytes 18440 | tf_op jit(solution)/shard_map/ppermute | solution.py:21
Sparse Core Ops, SparseCore 0:
  19.4 141.6 all-reduce.1
where the time goes:
time: 1030 us; the launch traced here: 1020 us
  other arithmetic  587 us (57%)
  local copies, waits for them, and re-layouts  227 us (22%)
  waiting for transfers between devices  156 us (15%)
  starting transfers between devices  22.1 us (2%)
  between operations  14.6 us (1%)
    reduce_sum x128, other arithmetic, dipole_kernel(): jnp.sum(weight[None] * (0.25 * displace * projected[None] - 0.5 * spread_...  199 us
    psum x1, waiting for transfers between devices, per_device(): centroid = lax.psum(coords, 'bead') / beads  145 us
    reduce_sum x128, other arithmetic, dipole_kernel(): weight = jnp.exp(-0.25 * jnp.sum(displace * displace, axis=0))  135 us
    exp x128, other arithmetic, dipole_kernel(): weight = jnp.exp(-0.25 * jnp.sum(displace * displace, axis=0))  119 us
    sub x256, local copies, waits for them, and re-layouts, dipole_kernel(): displace = targets[:, :, :, None] - sources[:, :, None, :]  105 us
    sub x64, local copies, waits for them, and re-layouts, repulsion_kernel(): displace = targets[:, :, :, None] - sources[:, :, None, :]  48 us
    gather x8, local copies, waits for them, and re-layouts, gather_local(): picked = jnp.take(tiles, tile_rows, axis=1)  29.6 us
    reduce_sum x32, other arithmetic, repulsion_kernel(): return REPULSION * jnp.sum(weight[None] * displace, axis=3)  27.5 us
  transfers between devices with their start and end apart: 15, of which 5 were waited for; matrix products, arithmetic and copies ran while one was open for 55% of the time, Pallas kernels for 0%

commit v1 on v0

--- a/solution.py
+++ b/solution.py
@@ -83,7 +83,7 @@
     short_range = grouped(repulsion_kernel, targets, (gather_local(extended, neighbors),)).reshape(
         3, atom_dev
     )
-    centroid = lax.psum(coords, "bead") / beads
+    centroid = jnp.sum(lax.all_gather(coords, "bead"), axis=0) / beads
     with_charge = jnp.concatenate([centroid, charges[None]], axis=0)
     cent_ext = extended_2(with_charge, (("space", 1),), rim_width)
     cent_tiles = centroid.reshape(3, tiles_domain, TILE)

time: 1030 us -> 976 us (0.948)
  waiting for transfers between devices: 156 us -> 103 us
    psum x1 -> x0, waiting for transfers between devices: 145 us -> none  [per_device(): centroid = lax.psum(coords, 'bead') / beads]
    all_gather x0 -> x1, waiting for transfers between devices: none -> 95.8 us  [per_device(): centroid = jnp.sum(lax.all_gather(coords, 'bead'), axis=0) / beads]
  transfers between devices with their start and end apart: 15 -> 15, of which waited for: 5 -> 5; matrix products, arithmetic and copies ran while one was open for 55% -> 58% of each run, Pallas kernels for 0% -> 0%
where the time goes in v1:
time: 976 us; the launch traced here: 964 us
  other arithmetic  591 us (61%)
  local copies, waits for them, and re-layouts  228 us (23%)
  waiting for transfers between devices  103 us (11%)
  starting transfers between devices  18 us (2%)
  between operations  14.6 us (1%)
    reduce_sum x128, other arithmetic, dipole_kernel(): jnp.sum(weight[None] * (0.25 * displace * projected[None] - 0.5 * spread_...  199 us
    reduce_sum x128, other arithmetic, dipole_kernel(): weight = jnp.exp(-0.25 * jnp.sum(displace * displace, axis=0))  135 us
    exp x128, other arithmetic, dipole_kernel(): weight = jnp.exp(-0.25 * jnp.sum(displace * displace, axis=0))  119 us
    sub x256, local copies, waits for them, and re-layouts, dipole_kernel(): displace = targets[:, :, :, None] - sources[:, :, None, :]  105 us
    all_gather x1, waiting for transfers between devices, per_device(): centroid = jnp.sum(lax.all_gather(coords, 'bead'), axis=0) / beads  95.8 us
    sub x64, local copies, waits for them, and re-layouts, repulsion_kernel(): displace = targets[:, :, :, None] - sources[:, :, None, :]  48 us
    gather x8, local copies, waits for them, and re-layouts, gather_local(): picked = jnp.take(tiles, tile_rows, axis=1)  29.6 us
    reduce_sum x32, other arithmetic, charge_kernel(): return jnp.sum(weight[None] * displace, axis=3)  27.5 us
  transfers between devices with their start and end apart: 15, of which 5 were waited for; matrix products, arithmetic and copies ran while one was open for 58% of the time, Pallas kernels for 0%

profile of v1, /device:TPU:7, one launch (start us, length us, event | category | flops | bytes accessed | tf_op | source)
XLA Modules:
  0.0 963.9 jit_solution(5654028894666897079)
XLA Ops:
  7.2 1.8 copy.179
  9.7 2.5 collective-permute-start
  14.9 95.8 %all-gather.2.cloned.1.call-done = f32[32,3,16384]{2,1,0:T(4,128)} async-done(((f32[1,3,16384]{2,1,0:T(4,128)}), f32[32,3,16384]{2,1,0:T(4,128)}) %all-gather.2.cloned.1.call-update) | async-done | bytes 6291472 | tf_op jit(solution)/shard_map/all_gather | solution.py:86
  110.6 4.8 reduce_sum.153
  115.5 1.6 collective-permute-start.4
  117.1 3.6 gather_fusion.1
  121.6 2.8 gather_fusion
  125.4 8.0 gather_fusion.2
  133.4 3.6 fusion.29
  137.0 1.8 reshape_reshape.47
  140.4 87.0 %while.61 = (s32[]{:T(128)}, f32[32,3,4,128]{3,2,1,0:T(4,128)S(1)}, f32[32,3,4,128]{3,2,1,0:T(4,128)S(1)}, f32[32,3,4,1024]{3,2,1,0:T(4,128)}, f32[32,1,4,1024]{3,2,1,0:T(4,128)S(1)}, /*index=5*/s32[]{:T(128)}) while((s32[]{:T(128)}, f32[32,3,4,128]{3,2,1,0:T(4,128)S(1)}, f32[32,3,4,128]{3,2,1,0:T(4,128)S(1)}, f32[32,3,4,1024]{3,2,1,0:T(4,128)}, ...), condition=%wide.region_8.10_spmd, body=%wide.region_5.9_spmd.sunk | while | flops 9959938 | bytes 8677469 | solution.py:59
  227.7 2.6 collective-permute-start.6
  231.1 3.5 collective-permute-done.7
  234.6 3.6 gather_fusion.3
  239.6 1.8 reshape_reshape.49
  241.4 141.8 %while.62 = (s32[]{:T(128)}, f32[32,3,4,128]{3,2,1,0:T(4,128)S(1)}, f32[32,3,4,128]{3,2,1,0:T(4,128)S(1)}, f32[32,3,4,1024]{3,2,1,0:T(4,128)}, f32[32,3,4,1024]{3,2,0,1:T(4,128)S(1)}, /*index=5*/s32[]{:T(128)}) while((s32[]{:T(128)}, f32[32,3,4,128]{3,2,1,0:T(4,128)S(1)}, f32[32,3,4,128]{3,2,1,0:T(4,128)S(1)}, ...), condition=%wide.region_13.15_spmd, body=%wide.region_9.14_spmd.sunk | while | flops 15739394 | bytes 17262684 | solution.py:59
  384.1 4.8 collective-permute-start.3
  389.0 3.6 gather_fusion.4
  393.9 1.8 reshape_reshape.51
  395.8 141.8 %while.63 = (s32[]{:T(128)}, f32[32,3,4,128]{3,2,1,0:T(4,128)S(1)}, f32[32,3,4,128]{3,2,1,0:T(4,128)S(1)}, f32[32,3,4,1024]{3,2,1,0:T(4,128)}, f32[32,3,4,1024]{3,2,0,1:T(4,128)S(1)}, /*index=5*/s32[]{:T(128)}) while((s32[]{:T(128)}, f32[32,3,4,128]{3,2,1,0:T(4,128)S(1)}, f32[32,3,4,128]{3,2,1,0:T(4,128)S(1)}, ...), condition=%wide.region_18.20_spmd, body=%wide.region_14.19_spmd.sunk | while | flops 15739394 | bytes 17262684 | solution.py:59
  537.9 3.1 collective-permute-start.10
  541.0 1.7 reshape_reshape.45
  542.7 2.6 collective-permute-done.11
  545.3 3.6 gather_fusion.5
  550.3 1.8 reshape_reshape.53
  552.1 141.8 %while.64 = (s32[]{:T(128)}, f32[32,3,4,128]{3,2,1,0:T(4,128)S(1)}, f32[32,3,4,128]{3,2,1,0:T(4,128)S(1)}, f32[32,3,4,1024]{3,2,1,0:T(4,128)}, f32[32,3,4,1024]{3,2,0,1:T(4,128)S(1)}, /*index=5*/s32[]{:T(128)}) while((s32[]{:T(128)}, f32[32,3,4,128]{3,2,1,0:T(4,128)S(1)}, f32[32,3,4,128]{3,2,1,0:T(4,128)S(1)}, ...), condition=%wide.region_23.25_spmd, body=%wide.region_19.24_spmd.sunk | while | flops 15739394 | bytes 17262684 | solution.py:59
  694.8 3.0 collective-permute-start.12
  697.8 107.9 %while.60 = (s32[]{:T(128)}, f32[32,3,4,128]{3,2,1,0:T(4,128)S(1)}, f32[32,3,4,128]{3,2,0,1:T(4,128)}, f32[32,3,4,1024]{3,2,0,1:T(4,128)}, s32[]{:T(128)}) while((s32[]{:T(128)}, f32[32,3,4,128]{3,2,1,0:T(4,128)S(1)}, f32[32,3,4,128]{3,2,0,1:T(4,128)}, f32[32,3,4,1024]{3,2,0,1:T(4,128)}, s32[]{:T(128)}) %tuple.172), condition=%wide.region_3.5_spmd, body=%wide.region_0.4_spmd.sunk | while | flops 9437186 | bytes 8628305 | solution.py:59
  805.9 3.6 gather_fusion.6
  810.9 1.8 reshape_reshape.55
  812.7 142.0 %while.65 = (s32[]{:T(128)}, f32[32,3,4,128]{3,2,1,0:T(4,128)S(1)}, f32[32,3,4,128]{3,2,1,0:T(4,128)S(1)}, f32[32,3,4,1024]{3,2,1,0:T(4,128)}, f32[32,3,4,1024]{3,2,0,1:T(4,128)S(1)}, /*index=5*/s32[]{:T(128)}) while((s32[]{:T(128)}, f32[32,3,4,128]{3,2,1,0:T(4,128)S(1)}, f32[32,3,4,128]{3,2,1,0:T(4,128)S(1)}, ...), condition=%wide.region_28.30_spmd, body=%wide.region_24.29_spmd.sunk | while | flops 15739394 | bytes 17262684 | solution.py:59
  954.8 2.2 multiply_add_fusion
  (1401 shorter events, 769.2 us)
Async XLA Ops:
  7.2 103.5 %all-gather.2.cloned.1.call-start = ((), (), s32[]{:S(2)}) async-start(), calls=%async_computation | async-start | bytes 8650752 | tf_op jit(solution)/shard_map/all_gather | solution.py:86
  9.7 107.3 %collective-permute-start = (f32[3,512]{1,0:T(4,128)S(1)}, f32[3,512]{1,0:T(4,128)S(1)}, u32[]{:S(2)}, u32[]{:S(2)}) collective-permute-start(f32[3,512]{1,0:T(4,128)S(1)} %get-tuple-element.340), channel_id=1, source_target_pairs={{0,1},{1,2},{2,3},{3,4},{4,5},{5,6},{6,7},{7,0},{8,9},{9,10},{10,1... | collective-permute-start | bytes 18440 | tf_op jit(solution)/shard_map/ppermute | solution.py:21
  12.2 104.9 %collective-permute-start.1 = (f32[3,512]{1,0:T(4,128)S(1)}, f32[3,512]{1,0:T(4,128)S(1)}, u32[]{:S(2)}, u32[]{:S(2)}) collective-permute-start(f32[3,512]{1,0:T(4,128)S(1)} %get-tuple-element.341), channel_id=1, source_target_pairs={{1,0},{2,1},{3,2},{4,3},{5,4},{6,5},{7,6},{0,7},{9,8},{10,9},{11,1... | collective-permute-start | bytes 18440 | tf_op jit(solution)/shard_map/ppermute | solution.py:22
  14.9 100.6 %copy-start.3 = (f32[16384]{0:T(1024)S(1)}, f32[16384]{0:T(1024)}, u32[]{:S(2)}) copy-start(f32[16384]{0:T(1024)} %param.20) | copy-start | bytes 196612
  14.9 102.2 %copy-start.1 = (f32[1,3,16384]{2,1,0:T(4,128)S(1)}, f32[1,3,16384]{2,1,0:T(4,128)}, u32[]{:S(2)}) copy-start(f32[1,3,16384]{2,1,0:T(4,128)} %copy.179) | copy-start | bytes 589828
  115.5 5.5 collective-permute-start.4
  117.1 4.3 collective-permute-start.5
  138.8 1.3 copy-start.2
  138.8 1.3 copy-start.5
  140.4 87.2 %copy-start.4 = (f32[16384]{0:T(1024)S(1)}, f32[16384]{0:T(1024)}, u32[]{:S(2)}) copy-start(f32[16384]{0:T(1024)} %param.21) | copy-start | bytes 196612
  227.7 3.4 collective-permute-start.6
  230.3 4.3 collective-permute-start.7
  383.6 5.3 collective-permute-start.8
  383.6 5.3 collective-permute-start.9
  384.1 570.7 %collective-permute-start.2 = (f32[1,3,16384]{2,0,1:T(1,128)}, f32[1,3,16384]{2,0,1:T(1,128)S(1)}, u32[]{:S(2)}, u32[]{:S(2)}) collective-permute-start(f32[1,3,16384]{2,0,1:T(1,128)} %param.19), channel_id=1, source_target_pairs={{0,8},{8,16},{16,24},{24,32},{32,40},{40,48},{48,56},{56,64},{64,7... | collective-permute-start | bytes 589832 | tf_op jit(solution)/shard_map/ppermute | solution.py:21
  384.1 570.7 %collective-permute-start.3 = (f32[1,3,16384]{2,0,1:T(1,128)}, f32[1,3,16384]{2,0,1:T(1,128)}, u32[]{:S(2)}, u32[]{:S(2)}) collective-permute-start(f32[1,3,16384]{2,0,1:T(1,128)} %param.19), channel_id=1, source_target_pairs={{8,0},{16,8},{24,16},{32,24},{40,32},{48,40},{56,48},{64,56},{72,6... | collective-permute-start | bytes 589832 | tf_op jit(solution)/shard_map/ppermute | solution.py:22
  395.8 145.2 %copy-start.6 = (f32[16384]{0:T(1024)S(1)}, f32[16384]{0:T(1024)}, u32[]{:S(2)}) copy-start(f32[16384]{0:T(1024)} %param.22) | copy-start | bytes 196612
  537.6 3.4 copy-start
  537.9 4.7 collective-permute-start.10
  541.0 4.3 collective-permute-start.11
  694.8 111.0 %collective-permute-start.13 = (f32[3,512]{1,0:T(4,128)S(1)}, f32[3,512]{1,0:T(4,128)S(1)}, u32[]{:S(2)}, u32[]{:S(2)}) collective-permute-start(f32[3,512]{1,0:T(4,128)S(1)} %get-tuple-element.338), channel_id=1, source_target_pairs={{1,0},{2,1},{3,2},{4,3},{5,4},{6,5},{7,6},{0,7},{9,8},{10,9},{11,1... | collective-permute-start | bytes 18440 | tf_op jit(solution)/shard_map/ppermute | solution.py:22
  694.8 111.0 %collective-permute-start.12 = (f32[3,512]{1,0:T(4,128)S(1)}, f32[3,512]{1,0:T(4,128)S(1)}, u32[]{:S(2)}, u32[]{:S(2)}) collective-permute-start(f32[3,512]{1,0:T(4,128)S(1)} %get-tuple-element.339), channel_id=1, source_target_pairs={{0,1},{1,2},{2,3},{3,4},{4,5},{5,6},{6,7},{7,0},{8,9},{9,10},{10,1... | collective-permute-start | bytes 18440 | tf_op jit(solution)/shard_map/ppermute | solution.py:21
Sparse Core Ops, SparseCore 0:
  10.6 100.0 all-gather.1
